TPU v7x, 32 devices: a whole 2x2x4 slice. The times are simulated.
32 devices in a mesh: table: 16 (over z, y, x), ctx: 2 (over core).
Axes of the slice: x: 2, y: 2, z: 4, core: 2. Of those that a mesh axis runs over, the one named last changes fastest.
Arguments:
- item_table: float32 [32768, 256], P('table'), may hold values from -3 to 3
- serve_rows: int32 [256, 512], P('table', 'ctx'), may hold values from 0 to 2047, as said below
- token_slots: int32 [16, 2048, 4], P('table', 'ctx'), may hold values from 0 to 4095
- lengths: int32 [16], P('table'), may hold values from 1 to 2048, as said below
- w_proj: bfloat16 [256, 2048], replicated, may hold values from -0.375 to 0.375
- w_out: bfloat16 [512, 256], replicated, may hold values from -0.25 to 0.25
- grad_out: bfloat16 [16, 2048, 256], P('table', 'ctx'), may hold values from -6 to 6
Outputs:
- layer_out: bfloat16 [16, 2048, 256], P('table', 'ctx')
- grad_table: float32 [32768, 256], P(('table', 'ctx'))
Inputs may be any that keep to these rules, and one draw needn't show every extreme that they name: `serve_rows`: the 256 rows that one owner serves to one requesting device are distinct. `lengths`: some history has all 2048 actions.
All inputs are finite; a program needn't handle non-finite values.
Results may differ from a plain program's by a relative error of at most 0.009.
Values may be sent and summed in bfloat16 or wider, within the bound.
No kernel may reach another device: no remote copies, remote signals or barrier semaphores. Data moves between devices by JAX's collectives and lax.ppermute only.
A program may use at most 192 MiB of HBM per device.

v0:
```python
import jax
import jax.numpy as jnp
from jax import lax
from jax.sharding import PartitionSpec as P

HEAD = 128


epsilon = 1e-05
block_rows = 512


def silu_slope(inputs):
    sigmoid_value = jax.nn.sigmoid(inputs)
    return sigmoid_value * (1.0 + inputs * (1.0 - sigmoid_value))


def normalize(inputs):
    centred = inputs - jnp.mean(inputs, axis=-1, keepdims=True)
    inverse = lax.rsqrt(jnp.mean(centred * centred, axis=-1, keepdims=True) + epsilon)
    return (centred * inverse, inverse)


def norm_back(gradients, normed, inverse):
    return (
        gradients
        - jnp.mean(gradients, axis=-1, keepdims=True)
        - normed * jnp.mean(gradients * normed, axis=-1, keepdims=True)
    ) * inverse


def blockwise(step_fn, carried, pieces, first_row):
    row_total = pieces[0].shape[0]

    def visit_block(step_index, current):
        offset = step_index * block_rows
        subset = tuple(
            (lax.dynamic_slice_in_dim(one_piece, offset, block_rows, 0) for one_piece in pieces)
        )
        return step_fn(current, subset, first_row + offset)

    return lax.fori_loop(0, row_total // block_rows, visit_block, carried)


def split_heads(matrix):
    return matrix.reshape(matrix.shape[0], -1, HEAD)


def scores(query_rows, key_rows):
    return jnp.einsum(
        "ihd,jhd->hij",
        split_heads(query_rows),
        split_heads(key_rows),
        preferred_element_type=jnp.float32,
    ) * HEAD ** (-0.5)


def on_device(item_table, serve_rows, token_slots, lengths, w_proj, w_out, grad_out):
    row_width = item_table.shape[1]
    served = item_table[serve_rows]
    fetched = lax.all_to_all(served, "table", split_axis=0, concat_axis=0, tiled=True)
    fetched_rows = fetched.reshape(-1, row_width)
    slot_ids = token_slots[0]
    embedded = fetched_rows[slot_ids[:, 0]]
    for feature in range(1, slot_ids.shape[1]):
        embedded = embedded + fetched_rows[slot_ids[:, feature]]
    row_count = embedded.shape[0]
    length = lengths[0]
    first_pos = lax.axis_index("ctx") * row_count
    positions = first_pos + jnp.arange(row_count, dtype=jnp.int32)
    valid_rows = positions < length
    score_scale = HEAD ** (-0.5)
    hidden_full = w_out.shape[0]
    normal_x, input_inverse = normalize(embedded)
    normed_input = normal_x.astype(jnp.bfloat16)
    cotangent = grad_out[0]
    masked_g = jnp.where(valid_rows[:, None], cotangent, jnp.zeros_like(cotangent))

    def allowed(query_pos, key_pos):
        return ((key_pos[None, :] <= query_pos[:, None]) & (key_pos[None, :] < length)).astype(
            jnp.float32
        )

    def key_terms(query_block, grad_block, key_block, value_block, query_pos, key_pos):
        key_total = key_block.shape[0]
        block_width = key_block.shape[1]
        scaled = scores(query_block, key_block)
        allowed_mask = allowed(query_pos, key_pos)
        weights = (jax.nn.silu(scaled) * allowed_mask).astype(jnp.bfloat16)
        grad_v = jnp.einsum(
            "hij,ihd->jhd", weights, split_heads(grad_block), preferred_element_type=jnp.float32
        )
        grad_weights = jnp.einsum(
            "ihd,jhd->hij",
            split_heads(grad_block),
            split_heads(value_block),
            preferred_element_type=jnp.float32,
        )
        grad_scores = (grad_weights * silu_slope(scaled) * score_scale * allowed_mask).astype(
            jnp.bfloat16
        )
        grad_k = jnp.einsum(
            "hij,ihd->jhd",
            grad_scores,
            split_heads(query_block),
            preferred_element_type=jnp.float32,
        )
        grad_q = jnp.einsum(
            "hij,jhd->ihd", grad_scores, split_heads(key_block), preferred_element_type=jnp.float32
        )
        return (
            grad_q.reshape(query_block.shape[0], block_width),
            grad_k.reshape(key_total, block_width),
            grad_v.reshape(key_total, block_width),
        )

    head_total = hidden_full // HEAD
    share = head_total // lax.axis_size("ctx")
    head_start = lax.axis_index("ctx") * share
    proj_cols = lax.dynamic_slice_in_dim(
        w_proj.reshape(row_width, 4, head_total, HEAD), head_start, share, 2
    ).reshape(row_width, 4 * share * HEAD)
    out_rows = lax.dynamic_slice_in_dim(
        w_out.reshape(head_total, HEAD, row_width), head_start, share, 0
    ).reshape(share * HEAD, row_width)
    inputs_all, cotangent_all = (
        lax.all_gather(normed_input, "ctx", axis=0, tiled=True),
        lax.all_gather(cotangent, "ctx", axis=0, tiled=True),
    )
    all_total = inputs_all.shape[0]
    all_pos = jnp.arange(all_total, dtype=jnp.int32)
    all_valid = all_pos < length
    pre_mine = jnp.dot(inputs_all, proj_cols, preferred_element_type=jnp.float32)
    act_mine = jax.nn.silu(pre_mine).astype(jnp.bfloat16)
    gating_m, values_m, queries_m, keys_m = jnp.split(act_mine, 4, axis=1)
    width_mine = values_m.shape[1]

    def attend_all(current, subset, first_row):
        key_block, value_block = subset
        key_pos = first_row + jnp.arange(key_block.shape[0], dtype=jnp.int32)
        weights = (jax.nn.silu(scores(queries_m, key_block)) * allowed(all_pos, key_pos)).astype(
            jnp.bfloat16
        )
        summed = jnp.einsum(
            "hij,jhd->ihd", weights, split_heads(value_block), preferred_element_type=jnp.float32
        )
        return current + summed.reshape(all_total, width_mine)

    attended_m = blockwise(
        attend_all, jnp.zeros((all_total, width_mine), jnp.float32), (keys_m, values_m), 0
    )
    row_sum, row_squares = lax.psum(
        (jnp.sum(attended_m, axis=1), jnp.sum(attended_m * attended_m, axis=1)), "ctx"
    )
    middle = (row_sum / hidden_full)[:, None]
    out_inverse = lax.rsqrt((row_squares / hidden_full)[:, None] - middle * middle + epsilon)
    normed_m = (attended_m - middle) * out_inverse
    gated_m = (normed_m * gating_m.astype(jnp.float32)).astype(jnp.bfloat16)
    mixed_rows = lax.psum_scatter(
        jnp.dot(gated_m, out_rows, preferred_element_type=jnp.float32).astype(jnp.bfloat16),
        "ctx",
        scatter_dimension=0,
        tiled=True,
    ).astype(jnp.float32)
    layer_out = jnp.where(valid_rows[:, None], embedded + mixed_rows, 0.0).astype(jnp.bfloat16)
    masked_all = jnp.where(all_valid[:, None], cotangent_all, jnp.zeros_like(cotangent_all))
    grad_gated_m = jnp.einsum("td,hd->th", masked_all, out_rows, preferred_element_type=jnp.float32)
    grad_gating_m = grad_gated_m * normed_m
    t_rows = grad_gated_m * gating_m.astype(jnp.float32)
    t_sum, tn_sum = lax.psum((jnp.sum(t_rows, axis=1), jnp.sum(t_rows * normed_m, axis=1)), "ctx")
    grad_att_m = (
        (t_rows - (t_sum / hidden_full)[:, None] - normed_m * (tn_sum / hidden_full)[:, None])
        * out_inverse
    ).astype(jnp.bfloat16)

    def back_block(step_index, carried):
        first_row = step_index * block_rows
        key_block = lax.dynamic_slice_in_dim(keys_m, first_row, block_rows, 0)
        value_block = lax.dynamic_slice_in_dim(values_m, first_row, block_rows, 0)
        key_pos = first_row + jnp.arange(block_rows, dtype=jnp.int32)
        more_q, more_k, more_v = key_terms(
            queries_m, grad_att_m, key_block, value_block, all_pos, key_pos
        )
        return (
            carried[0] + more_q,
            lax.dynamic_update_slice_in_dim(carried[1], more_k, first_row, 0),
            lax.dynamic_update_slice_in_dim(carried[2], more_v, first_row, 0),
        )

    zero_all = jnp.zeros((all_total, width_mine), jnp.float32)
    grad_q_m, grad_k_m, grad_v_m = lax.fori_loop(
        0, all_total // block_rows, back_block, (zero_all, zero_all, zero_all)
    )
    grad_act_m = jnp.concatenate([grad_gating_m, grad_v_m, grad_q_m, grad_k_m], axis=1)
    grad_pre_m = (grad_act_m * silu_slope(pre_mine)).astype(jnp.bfloat16)
    grad_x = lax.psum_scatter(
        jnp.einsum("tp,dp->td", grad_pre_m, proj_cols, preferred_element_type=jnp.float32).astype(
            jnp.bfloat16
        ),
        "ctx",
        scatter_dimension=0,
        tiled=True,
    ).astype(jnp.float32)
    grad_emb = masked_g.astype(jnp.float32) + norm_back(grad_x, normal_x, input_inverse)
    spread = jnp.broadcast_to(
        grad_emb[:, None, :], (row_count, slot_ids.shape[1], row_width)
    ).reshape(-1, row_width)
    slot_grads = jax.ops.segment_sum(
        spread, slot_ids.reshape(-1), num_segments=fetched_rows.shape[0]
    )
    returned = lax.all_to_all(
        slot_grads.reshape(fetched.shape).astype(jnp.bfloat16),
        "table",
        split_axis=0,
        concat_axis=0,
        tiled=True,
    ).astype(jnp.float32)
    owner_grads = jax.ops.segment_sum(
        returned.reshape(-1, row_width), serve_rows.reshape(-1), num_segments=item_table.shape[0]
    )
    grad_table = lax.psum_scatter(
        owner_grads.astype(jnp.bfloat16), "ctx", scatter_dimension=0, tiled=True
    ).astype(jnp.float32)
    return (layer_out[None], grad_table)


def solution(mesh):
    placed = (
        P("table", None),
        P("table", "ctx"),
        P("table", "ctx", None),
        P("table"),
        P(),
        P(),
        P("table", "ctx", None),
    )
    return jax.shard_map(
        on_device,
        mesh=mesh,
        in_specs=placed,
        out_specs=(P("table", "ctx", None), P(("table", "ctx"), None)),
        check_vma=False,
    )
```

profile of v0, /device:TPU:15, one launch (start us, length us, event | category | flops | bytes accessed | tf_op | source)
XLA Modules:
  0.0 506.3 jit_solution(6258726801934168337)
XLA Ops:
  8.8 16.2 %gather_fusion = f32[4096,256]{1,0:T(8,128)} fusion(f32[2048,256]{1,0:T(8,128)S(1)} %copy-done, s32[4096]{0:T(1024)S(1)} %broadcast_clamp_fusion), kind=kCustom, calls=%fused_computation | custom fusion | bytes 8404992 | tf_op jit(solution)/shard_map/gather | solution.py:60
  25.0 6.7 %all-to-all-start = ((f32[16,256,256]{2,1,0:T(8,128)}), f32[16,256,256]{2,1,0:T(8,128)}, u32[]{:S(2)}, u32[]{:S(2)}) async-start(f32[16,256,256]{2,1,0:T(8,128)} %bitcast.183), calls=%async_computation | async-start | bytes 8388608 | tf_op jit(solution)/shard_map/all_to_all | solution.py:61
  31.9 94.5 %all-to-all-done = f32[16,256,256]{2,1,0:T(8,128)} async-done(((f32[16,256,256]{2,1,0:T(8,128)}), f32[16,256,256]{2,1,0:T(8,128)}, u32[]{:S(2)}, u32[]{:S(2)}) %all-to-all-start) | async-done | bytes 4194336 | tf_op jit(solution)/shard_map/all_to_all | solution.py:61
  126.3 5.6 %gather_fusion.4 = f32[1024,256]{1,0:T(8,128)S(1)} fusion(f32[4096,256]{1,0:T(8,128)} %bitcast.2, s32[1024]{0:T(1024)S(1)} %broadcast_clamp_fusion.1), kind=kCustom, calls=%fused_computation.4 | custom fusion | bytes 2101248 | tf_op jit(solution)/shard_map/gather | solution.py:66
  132.0 5.6 %gather_fusion.3 = f32[1024,256]{1,0:T(8,128)S(1)} fusion(f32[4096,256]{1,0:T(8,128)} %bitcast.2, s32[1024]{0:T(1024)S(1)} %broadcast_clamp_fusion.2), kind=kCustom, calls=%fused_computation.3 | custom fusion | bytes 2101248 | tf_op jit(solution)/shard_map/gather | solution.py:66
  137.7 5.6 %gather_fusion.2 = f32[1024,256]{1,0:T(8,128)S(1)} fusion(f32[4096,256]{1,0:T(8,128)} %bitcast.2, s32[1024]{0:T(1024)S(1)} %broadcast_clamp_fusion.3), kind=kCustom, calls=%fused_computation.2 | custom fusion | bytes 2101248 | tf_op jit(solution)/shard_map/gather | solution.py:66
  143.3 6.9 %gather_fusion.1 = f32[1024,256]{1,0:T(8,128)} fusion(f32[4096,256]{1,0:T(8,128)} %bitcast.2, s32[1024]{0:T(1024)S(1)} %broadcast_clamp_fusion.4), kind=kCustom, calls=%fused_computation.1 | custom fusion | bytes 2101248 | tf_op jit(solution)/shard_map/gather | solution.py:64
  164.1 5.9 %multiply_convert_fusion = (bf16[2048,1024]{0,1:T(8,128)(2,1)S(1)}, f32[2048,1024]{0,1:T(8,128)}) fusion(bf16[2048,256]{1,0:T(8,128)(2,1)} %all-gather.4.cloned.1.call-done, bf16[256,1024]{1,0:T(8,128)(2,1)S(1)} %reshape.258), kind=kOutput, calls=%fused_computation.58 | convolution fusion | flops 1084227584 | bytes 14155776 | tf_op jit(solution)/shard_map/dot_general | solution.py:133
  174.9 60.2 %while.32 = (s32[]{:T(128)}, f32[2048,256]{0,1:T(8,128)S(1)}, bf16[2048,256]{0,1:T(8,128)(2,1)}, bf16[2048,256]{0,1:T(8,128)(2,1)}, bf16[2048,256]{1,0:T(8,128)(...) while((s32[]{:T(128)}, f32[2048,256]{0,1:T(8,128)S(1)}, ...), condition=%wide.region_3.4_spmd.clone, body=%wide.region_2.3_spmd.clone.sunk | while | flops 1092617728 | bytes 19403956 | solution.py:42
  180.0 7.6 %fusion.117 = f32[2,128,2048]{2,1,0:T(8,128)} fusion(bf16[512,2,128]{0,2,1:T(8,128)(2,1)} %bitcast.187, bf16[512,2,128]{0,2,1:T(8,128)(2,1)S(1)} %bitcast.186, f32[2048,512]{0,1:T(8,128)} %fusion.116, bf16[2048,256]{1,0:T(8,128)(2,1)} %get-tuple-element.574), kind=kOutput, calls=%fused_computation.20.clone.1 | convolution fusion | flops 1088421888 | bytes 7864320 | tf_op jit(solution)/shard_map/while/body/eval_jaxpr/hij,jhd->ihd/dot_general | solution.py:144
  195.1 7.6 %fusion.117 = f32[2,128,2048]{2,1,0:T(8,128)} fusion(bf16[512,2,128]{0,2,1:T(8,128)(2,1)} %bitcast.187, bf16[512,2,128]{0,2,1:T(8,128)(2,1)S(1)} %bitcast.186, f32[2048,512]{0,1:T(8,128)} %fusion.116, bf16[2048,256]{1,0:T(8,128)(2,1)} %get-tuple-element.574), kind=kOutput, calls=%fused_computation.20.clone.1 | convolution fusion | flops 1088421888 | bytes 7864320 | tf_op jit(solution)/shard_map/while/body/eval_jaxpr/hij,jhd->ihd/dot_general | solution.py:144
  210.2 7.6 %fusion.117 = f32[2,128,2048]{2,1,0:T(8,128)} fusion(bf16[512,2,128]{0,2,1:T(8,128)(2,1)} %bitcast.187, bf16[512,2,128]{0,2,1:T(8,128)(2,1)S(1)} %bitcast.186, f32[2048,512]{0,1:T(8,128)} %fusion.116, bf16[2048,256]{1,0:T(8,128)(2,1)} %get-tuple-element.574), kind=kOutput, calls=%fused_computation.20.clone.1 | convolution fusion | flops 1088421888 | bytes 7864320 | tf_op jit(solution)/shard_map/while/body/eval_jaxpr/hij,jhd->ihd/dot_general | solution.py:144
  225.2 7.6 %fusion.117 = f32[2,128,2048]{2,1,0:T(8,128)} fusion(bf16[512,2,128]{0,2,1:T(8,128)(2,1)} %bitcast.187, bf16[512,2,128]{0,2,1:T(8,128)(2,1)S(1)} %bitcast.186, f32[2048,512]{0,1:T(8,128)} %fusion.116, bf16[2048,256]{1,0:T(8,128)(2,1)} %get-tuple-element.574), kind=kOutput, calls=%fused_computation.20.clone.1 | convolution fusion | flops 1088421888 | bytes 7864320 | tf_op jit(solution)/shard_map/while/body/eval_jaxpr/hij,jhd->ihd/dot_general | solution.py:144
  245.9 4.2 fusion.46
  253.4 85.7 %while.33 = (s32[]{:T(128)}, f32[2048,256]{0,1:T(8,128)}, f32[2048,256]{0,1:T(8,128)}, f32[2048,256]{0,1:T(8,128)}, bf16[2048,256]{0,1:T(8,128)(2,1)}, /*index=5...) while((s32[]{:T(128)}, f32[2048,256]{0,1:T(8,128)}, ...), condition=%wide.region_14.15_spmd.clone, body=%wide.region_13.14_spmd.clone.sunk | while | flops 2729444864 | bytes 88874768 | solution.py:191
  260.9 4.5 fusion.133
  265.4 4.0 fusion.130
  282.3 4.5 fusion.133
  286.8 4.0 fusion.130
  303.7 4.5 fusion.133
  308.2 4.0 fusion.130
  325.2 4.5 fusion.133
  329.7 4.0 fusion.130
  339.1 8.9 %fusion.40 = bf16[2048,256]{1,0:T(8,128)(2,1)} fusion(bf16[256,1024]{1,0:T(8,128)(2,1)} %copy-done.12, f32[2048,256]{0,1:T(8,128)} %get-tuple-element.300, f32[2048,256]{0,1:T(8,128)} %get-tuple-element.299, f32[2048,256]{0,1:T(8,128)} %get-tuple-element.298, f32[2048,256]{0,1:T(8,128)} %get-tuple-element.432, f32[2048,1024]{0,1:T(8,128)} %get-tuple-element.446), kind=kOutput, calls=%fused_computation.65 | convolution fusion | flops 1099431936 | bytes 18350080 | tf_op jit(solution)/shard_map/tp,dp->td/dot_general | solution.py:197
  351.8 6.0 %reduce-scatter.6.cloned.1.call-done = bf16[1024,256]{1,0:T(8,128)(2,1)} async-done(((bf16[2048,256]{1,0:T(8,128)(2,1)}), bf16[1024,256]{1,0:T(8,128)(2,1)}) %reduce-scatter.6.cloned.1.call-update) | async-done | bytes 524304 | tf_op jit(solution)/shard_map/reduce_scatter | solution.py:196
  359.6 9.9 %reduce-scatter.4.cloned.1.call-done = bf16[1024,256]{1,0:T(8,128)(2,1)} async-done(((bf16[2048,256]{1,0:T(8,128)(2,1)}), bf16[1024,256]{1,0:T(8,128)(2,1)}) %reduce-scatter.4.cloned.1.call-update) | async-done | bytes 524304 | tf_op jit(solution)/shard_map/reduce_scatter | solution.py:159
  375.1 5.3 %reshape.310 = f32[4096,256]{1,0:T(8,128)} reshape(f32[1024,4,256]{2,1,0:T(4,128)} %broadcast_in_dim.91) | data formatting | bytes 8388608 | tf_op jit(solution)/shard_map/reshape | solution.py:207
  380.4 25.0 %scatter_custom_fusion = f32[4096,256]{1,0:T(8,128)} fusion(s32[4096]{0:T(1024)S(1)} %reshape.308, f32[4096,256]{1,0:T(8,128)} %reshape.310, f32[]{:T(128)} %constant.120.clone.1), kind=kCustom, calls=%fused_computation.70 | custom fusion | flops 1048576 | bytes 4194816 | tf_op jit(solution)/shard_map/scatter-add | solution.py:208
  409.2 6.4 %all-to-all-start.1 = ((bf16[16,256,256]{2,1,0:T(8,128)(2,1)}), bf16[16,256,256]{2,1,0:T(8,128)(2,1)}, u32[]{:S(2)}, u32[]{:S(2)}) async-start(bf16[16,256,256]{2,1,0:T(8,128)(2,1)} %bitcast.13), calls=%async_computation.3 | async-start | bytes 4194304 | tf_op jit(solution)/shard_map/all_to_all | solution.py:211
  415.7 47.9 %all-to-all-done.1 = bf16[16,256,256]{2,1,0:T(8,128)(2,1)} async-done(((bf16[16,256,256]{2,1,0:T(8,128)(2,1)}), bf16[16,256,256]{2,1,0:T(8,128)(2,1)}, u32[]{:S(2)}, u32[]{:S(2)}) %all-to-all-start.1) | async-done | bytes 2097184 | tf_op jit(solution)/shard_map/all_to_all | solution.py:211
  463.6 22.4 %scatter_custom_fusion.1 = f32[2048,256]{1,0:T(8,128)} fusion(s32[4096]{0:T(1024)S(1)} %bitcast.196, bf16[4096,256]{1,0:T(8,128)(2,1)} %bitcast.32, f32[]{:T(128)} %constant.120.clone.1), kind=kCustom, calls=%fused_computation.60 | custom fusion | flops 2097152 | bytes 4194308 | tf_op jit(solution)/shard_map/scatter-add | solution.py:218
  488.7 9.1 %reduce-scatter.8.cloned.1.call-done = bf16[1024,256]{1,0:T(8,128)(2,1)} async-done(((bf16[2048,256]{1,0:T(8,128)(2,1)}), bf16[1024,256]{1,0:T(8,128)(2,1)}) %reduce-scatter.8.cloned.1.call-update) | async-done | bytes 524304 | tf_op jit(solution)/shard_map/reduce_scatter | solution.py:221
  (181 shorter events, 134.5 us)
Async XLA Ops:
  7.2 1.6 copy-start
  25.0 6.8 %copy-start.21 = (s32[1,1024,4]{1,2,0:T(4,128)S(1)}, s32[1,1024,4]{1,2,0:T(4,128)}, u32[]{:S(2)}) copy-start(s32[1,1024,4]{1,2,0:T(4,128)} %param.13) | copy-start | bytes 49156
  25.0 101.3 %all-to-all-start = ((f32[16,256,256]{2,1,0:T(8,128)}), f32[16,256,256]{2,1,0:T(8,128)}, u32[]{:S(2)}, u32[]{:S(2)}) async-start(f32[16,256,256]{2,1,0:T(8,128)} %bitcast.183), calls=%async_computation | async-start | bytes 8388608 | tf_op jit(solution)/shard_map/all_to_all | solution.py:61
  31.7 132.4 %all-gather.4.cloned.1.call-start = ((), (), s32[]{:S(2)}) async-start(), calls=%async_computation.5 | async-start | bytes 1572864 | tf_op jit(solution)/shard_map/all_gather | solution.py:127
  151.7 6.0 %copy-start.23 = (bf16[512,256]{1,0:T(8,128)(2,1)S(1)}, bf16[512,256]{1,0:T(8,128)(2,1)}, u32[]{:S(2)}) copy-start(bf16[512,256]{1,0:T(8,128)(2,1)} %param.16) | copy-start | bytes 786436
  154.4 84.4 %all-gather.6.cloned.1.call-start = ((), (), s32[]{:S(2)}) async-start(), calls=%async_computation.9 | async-start | bytes 1572864 | tf_op jit(solution)/shard_map/all_gather | solution.py:128
  155.1 202.7 %reduce-scatter.6.cloned.1.call-start = ((), (), s32[]{:S(2)}) async-start(), calls=%async_computation.7 | async-start | bytes 1572864 | tf_op jit(solution)/shard_map/reduce_scatter | solution.py:196
  157.7 81.1 %copy-start.9 = (bf16[2,128,256]{2,1,0:T(8,128)(2,1)}, bf16[2,128,256]{2,1,0:T(8,128)(2,1)S(1)}, u32[]{:S(2)}) copy-start(bf16[2,128,256]{2,1,0:T(8,128)(2,1)S(1)} %constant_dynamic-slice_fusion.4) | copy-start | bytes 393220
  160.5 9.5 %copy-start.12 = (bf16[256,1024]{1,0:T(8,128)(2,1)}, bf16[256,1024]{1,0:T(8,128)(2,1)S(1)}, u32[]{:S(2)}) copy-start(bf16[256,1024]{1,0:T(8,128)(2,1)S(1)} %reshape.258) | copy-start | bytes 1572868
  170.0 2.0 copy-start.8
  235.1 10.8 %copy-start.2 = (f32[2048,256]{0,1:T(8,128)}, f32[2048,256]{0,1:T(8,128)S(1)}, u32[]{:S(2)}) copy-start(f32[2048,256]{0,1:T(8,128)S(1)} %get-tuple-element.297) | copy-start | bytes 6291460
  238.8 11.4 %copy-start.13 = (f32[2048]{0:T(1024)}, f32[2048]{0:T(1024)S(1)}, u32[]{:S(2)}) copy-start(f32[2048]{0:T(1024)S(1)} %get-tuple-element.443) | copy-start | bytes 24580
  238.8 11.4 %copy-start.15 = (f32[2048]{0:T(1024)}, f32[2048]{0:T(1024)S(1)}, u32[]{:S(2)}) copy-start(f32[2048]{0:T(1024)S(1)} %get-tuple-element.444) | copy-start | bytes 24580
  250.2 3.2 copy-start.11
  273.1 1.7 copy-start.5
  292.3 1.6 copy-start.4
  294.5 1.7 copy-start.5
  315.9 1.8 copy-start.5
  337.4 1.7 copy-start.5
  339.1 9.3 %copy-start.3 = (f32[2048,256]{0,1:T(8,128)S(1)}, f32[2048,256]{0,1:T(8,128)}, u32[]{:S(2)}) copy-start(f32[2048,256]{0,1:T(8,128)} %copy-done.2) | copy-start | bytes 6291460
  339.1 9.3 %copy-start.10 = (bf16[2,128,256]{2,1,0:T(8,128)(2,1)S(1)}, bf16[2,128,256]{2,1,0:T(8,128)(2,1)}, u32[]{:S(2)}) copy-start(bf16[2,128,256]{2,1,0:T(8,128)(2,1)} %copy-done.9) | copy-start | bytes 393220
  339.1 9.3 %copy-start.14 = (f32[2048]{0:T(1024)S(1)}, f32[2048]{0:T(1024)}, u32[]{:S(2)}) copy-start(f32[2048]{0:T(1024)} %copy-done.13) | copy-start | bytes 24580
  339.1 9.3 %copy-start.16 = (f32[2048]{0:T(1024)S(1)}, f32[2048]{0:T(1024)}, u32[]{:S(2)}) copy-start(f32[2048]{0:T(1024)} %copy-done.15) | copy-start | bytes 24580
  348.0 3.2 copy-start.22
  348.1 9.8 %copy-start.7 = (f32[1024,256]{1,0:T(8,128)S(1)}, f32[1024,256]{1,0:T(8,128)}, u32[]{:S(2)}) copy-start(f32[1024,256]{1,0:T(8,128)} %copy-done.6) | copy-start | bytes 3145732
  348.1 9.8 %copy-start.18 = (f32[1024]{0:T(1024)S(1)}, f32[1024]{0:T(1024)}, u32[]{:S(2)}) copy-start(f32[1024]{0:T(1024)} %copy-done.17) | copy-start | bytes 12292
  348.1 9.8 %copy-start.20 = (f32[1024]{0:T(1024)S(1)}, f32[1024]{0:T(1024)}, u32[]{:S(2)}) copy-start(f32[1024]{0:T(1024)} %copy-done.19) | copy-start | bytes 12292
  348.1 21.5 %reduce-scatter.4.cloned.1.call-start = ((), (), s32[]{:S(2)}) async-start(), calls=%async_computation.6 | async-start | bytes 1572864 | tf_op jit(solution)/shard_map/reduce_scatter | solution.py:159
  405.4 10.2 %copy-start.24 = (s32[16,256]{1,0:T(8,128)S(1)}, s32[16,256]{1,0:T(8,128)}, u32[]{:S(2)}) copy-start(s32[16,256]{1,0:T(8,128)} %param.12) | copy-start | bytes 49156
  409.2 54.4 %all-to-all-start.1 = ((bf16[16,256,256]{2,1,0:T(8,128)(2,1)}), bf16[16,256,256]{2,1,0:T(8,128)(2,1)}, u32[]{:S(2)}, u32[]{:S(2)}) async-start(bf16[16,256,256]{2,1,0:T(8,128)(2,1)} %bitcast.13), calls=%async_computation.3 | async-start | bytes 4194304 | tf_op jit(solution)/shard_map/all_to_all | solution.py:211
  415.6 82.1 %reduce-scatter.8.cloned.1.call-start = ((), (), s32[]{:S(2)}) async-start(), calls=%async_computation.8 | async-start | bytes 1572864 | tf_op jit(solution)/shard_map/reduce_scatter | solution.py:221
  463.6 36.3 %copy-start.1 = (f32[2048,256]{1,0:T(8,128)S(1)}, f32[2048,256]{1,0:T(8,128)}, u32[]{:S(2)}) copy-start(f32[2048,256]{1,0:T(8,128)} %param.11) | copy-start | bytes 6291460
  (6 other events, 7.3 us)
Sparse Core Ops, SparseCore 0:
  154.5 9.5 all-gather.3
  165.6 10.1 all-gather.5
  348.2 9.5 reduce-scatter.5
  359.9 9.5 reduce-scatter.3
  488.8 8.8 reduce-scatter.7
where the time goes:
time: 509 us; the launch traced here: 506 us
  waiting for transfers between devices  172 us (34%)
  other arithmetic  111 us (22%)
  matrix products  99.8 us (20%)
  local copies, waits for them, and re-layouts  88.2 us (17%)
  between operations  14.8 us (3%)
  starting transfers between devices  13.5 us (3%)
  blocking collectives  6.74 us (1%)
    all_to_all x1, waiting for transfers between devices, on_device(): lax.all_to_all(served, 'table', split_axis=0, concat_axis=0, tiled=True)  94.5 us
    all_to_all x1, waiting for transfers between devices, on_device(): lax.all_to_all(slot_grads.reshape(fetched.shape).astype(jnp.bfloat16), 't...  47.9 us
    dot_general x4, matrix products, attend_all(): jnp.einsum('hij,jhd->ihd', weights, split_heads(value_block), preferred_e...  30.4 us
    scatter-add x1, other arithmetic, on_device(): jax.ops.segment_sum(spread, slot_ids.reshape(-1), num_segments=fetched_ro...  25 us
    scatter-add x1, other arithmetic, on_device(): jax.ops.segment_sum(returned.reshape(-1, row_width), serve_rows.reshape(-...  22.4 us
    convert_element_type x8, other arithmetic, allowed(): ((key_pos[None, :] <= query_pos[:, None]) & (key_pos[None, :] < length))....  21.5 us
    dot_general x4, matrix products, key_terms(): jnp.einsum('hij,ihd->jhd', weights, split_heads(grad_block), preferred_el...  17.8 us
    gather x3, local copies, waits for them, and re-layouts, on_device(): embedded = embedded + fetched_rows[slot_ids[:, feature]]  16.9 us
  transfers between devices with their start and end apart: 7, of which 6 were waited for; matrix products, arithmetic and copies ran while one was open for 16% of the time, Pallas kernels for 0%

commit v1 on v0

v1 whole, which is shorter than its diff:
```python
import functools

import jax
import jax.numpy as jnp
from jax import lax
from jax.experimental import pallas as pl
from jax.experimental.pallas import tpu as pltpu
from jax.sharding import PartitionSpec as P

HEAD = 128
epsilon = 1e-05
F32 = jnp.float32
BF16 = jnp.bfloat16
ROWS = 256
BLOCK = 512


def mm(lhs, rhs):
    return lax.dot_general(lhs, rhs, (((1,), (0,)), ((), ())), preferred_element_type=F32)


def mm_rt(lhs, rhs):
    return lax.dot_general(lhs, rhs, (((1,), (1,)), ((), ())), preferred_element_type=F32)


def mm_lt(lhs, rhs):
    return lax.dot_general(lhs, rhs, (((0,), (0,)), ((), ())), preferred_element_type=F32)


def rows_at(start, count):
    return pl.ds(pl.multiple_of(start, count), count)


def vmem():
    return pl.BlockSpec(memory_space=pltpu.VMEM)


def smem():
    return pl.BlockSpec(memory_space=pltpu.SMEM)


def call(body, out_shape, in_specs, scratch=(), flops=0, moved=0):
    return pl.pallas_call(
        body,
        out_shape=out_shape,
        in_specs=in_specs,
        out_specs=jax.tree.map(lambda _: vmem(), out_shape),
        scratch_shapes=list(scratch),
        compiler_params=pltpu.CompilerParams(vmem_limit_bytes=60 * 1024 * 1024),
        cost_estimate=pl.CostEstimate(flops=flops, bytes_accessed=moved, transcendentals=0),
    )


def column(row, count):
    return jnp.transpose(jnp.broadcast_to(row, (HEAD, count)))


def serve_body(ids_ref, table_ref, out_ref, table_low, hot):
    table_low[...] = table_ref[...].astype(BF16)
    table_rows = table_ref.shape[0]
    lanes = lax.broadcasted_iota(jnp.int32, (BLOCK, HEAD), 1)

    def step(at, carry):
        ids = column(ids_ref[pl.ds(at, 1), :], BLOCK)
        for part in range(table_rows // HEAD):
            hit = ids == lanes + part * HEAD
            hot[:, part * HEAD : (part + 1) * HEAD] = jnp.where(hit, 1.0, 0.0).astype(BF16)
        out_ref[rows_at(at * BLOCK, BLOCK), :] = mm(hot[...], table_low[...]).astype(BF16)
        return carry

    lax.fori_loop(0, ids_ref.shape[0], step, 0)


def embed_body(slots_ref, fetched_ref, embedded_ref, normed_ref, hot):
    slot_total = fetched_ref.shape[0]
    lanes = lax.broadcasted_iota(jnp.int32, (ROWS, HEAD), 1)

    def step(at, carry):
        ids = [
            column(slots_ref[feature : feature + 1, rows_at(at * ROWS, ROWS)], ROWS)
            for feature in range(slots_ref.shape[0])
        ]
        for part in range(slot_total // HEAD):
            here = lanes + part * HEAD
            count = jnp.where(ids[0] == here, 1.0, 0.0)
            for one in ids[1:]:
                count = count + jnp.where(one == here, 1.0, 0.0)
            hot[:, part * HEAD : (part + 1) * HEAD] = count.astype(BF16)
        value = mm(hot[...], fetched_ref[...])
        where = rows_at(at * ROWS, ROWS)
        embedded_ref[where, :] = value
        normed_ref[where, :] = normalize(value)[0].astype(BF16)
        return carry

    lax.fori_loop(0, embedded_ref.shape[0] // ROWS, step, 0)


def normalize(inputs):
    centred = inputs - jnp.mean(inputs, axis=-1, keepdims=True)
    inverse = lax.rsqrt(jnp.mean(centred * centred, axis=-1, keepdims=True) + epsilon)
    return (centred * inverse, inverse)


def silu_parts(inputs):
    half = inputs * 0.5
    above = 1.0 + jnp.tanh(half)
    value = half * above
    return value, above


def slope_of(inputs):
    value, above = silu_parts(inputs)
    return 0.5 * above * (1.0 + inputs - value)


def forward_body(
    place_ref, xm_ref, xo_ref, gm_ref, go_ref, w_ref, wout_ref,
    x_ref, g_ref, act_ref, att_ref, stats_ref,
):
    mine, length = place_ref[0], place_ref[1]
    count = xm_ref.shape[0]
    total = x_ref.shape[0]
    width = att_ref.shape[1]
    x_ref[rows_at(mine * count, count), :] = xm_ref[...]
    x_ref[rows_at((1 - mine) * count, count), :] = xo_ref[...]
    g_ref[rows_at(mine * count, count), :] = gm_ref[...]
    g_ref[rows_at((1 - mine) * count, count), :] = go_ref[...]

    def project(at, carry):
        where = rows_at(at * ROWS, ROWS)
        value, _ = silu_parts(mm(x_ref[where, :], w_ref[...]))
        act_ref[where, :] = value.astype(BF16)
        below = at * ROWS + lax.broadcasted_iota(jnp.int32, (ROWS, g_ref.shape[1]), 0) < length
        g_ref[where, :] = jnp.where(below, g_ref[where, :].astype(F32), 0.0).astype(BF16)
        return carry

    lax.fori_loop(0, total // ROWS, project, 0)
    half_scale = 0.5 * HEAD ** (-0.5)

    def weigh(query, keys):
        half = mm_rt(query, keys) * half_scale
        return half * (1.0 + jnp.tanh(half))

    def attend(at, carry):
        def head_cols(kind, head):
            return pl.ds(kind * width + head * HEAD, HEAD)

        heads = range(width // HEAD)
        where = rows_at(at * BLOCK, BLOCK)
        queries = [act_ref[where, head_cols(2, head)] for head in heads]

        def visit(key_at, sums):
            keys_here = rows_at(key_at * BLOCK, BLOCK)
            new = []
            for head in heads:
                weights = weigh(queries[head], act_ref[keys_here, head_cols(3, head)]).astype(BF16)
                new.append(sums[head] + mm(weights, act_ref[keys_here, head_cols(1, head)]))
            return tuple(new)

        sums = lax.fori_loop(
            0, at, visit, tuple(jnp.zeros((BLOCK, HEAD), F32) for _ in heads)
        )
        for head in heads:
            for part in range(BLOCK // ROWS):
                seen = (part + 1) * ROWS
                query = queries[head][part * ROWS : seen]
                keys_here = pl.ds(pl.multiple_of(at * BLOCK, BLOCK), seen)
                weights = weigh(query, act_ref[keys_here, head_cols(3, head)])
                ok = lax.broadcasted_iota(jnp.int32, (ROWS, seen), 1) <= (
                    part * ROWS + lax.broadcasted_iota(jnp.int32, (ROWS, seen), 0)
                )
                weights = jnp.where(ok, weights, 0.0).astype(BF16)
                att_ref[rows_at(at * BLOCK + part * ROWS, ROWS), head_cols(0, head)] = sums[head][
                    part * ROWS : seen
                ] + mm(weights, act_ref[keys_here, head_cols(1, head)])
        return carry

    lax.fori_loop(0, total // BLOCK, attend, 0)

    def measure(at, carry):
        where = rows_at(at * ROWS, ROWS)
        attended = att_ref[where, :]
        gated_grad = mm_rt(g_ref[where, :], wout_ref[...])
        t_rows = gated_grad * act_ref[where, 0:width].astype(F32)
        lane = lax.broadcasted_iota(jnp.int32, (ROWS, HEAD), 1)
        sums = jnp.zeros((ROWS, HEAD), F32)
        for at_lane, one in enumerate(
            (attended, attended * attended, t_rows, t_rows * attended)
        ):
            sums = jnp.where(lane == at_lane, jnp.sum(one, axis=1, keepdims=True), sums)
        stats_ref[:, where] = jnp.transpose(sums)[0:8, :]
        return carry

    lax.fori_loop(0, total // ROWS, measure, 0)


def backward_body(
    place_ref, x_ref, g_ref, act_ref, att_ref, stats_m_ref, stats_o_ref, w_ref, wout_ref,
    mixed_m_ref, mixed_o_ref, gx_m_ref, gx_o_ref,
    datt_ref, dgate_ref, dq_ref, dk_ref, dv_ref,
):
    mine, length = place_ref[0], place_ref[1]
    count = mixed_m_ref.shape[0]
    total, width = att_ref.shape
    hidden = 2 * width

    def middle(at, out_at, mixed_ref):
        where = rows_at(at * ROWS, ROWS)
        stats = stats_m_ref[:, where] + stats_o_ref[:, where]
        stats = jnp.transpose(
            jnp.concatenate([stats, jnp.zeros((HEAD - 8, ROWS), F32)], axis=0)
        ) * (1.0 / hidden)
        mean = stats[:, 0:1]
        inverse = lax.rsqrt(stats[:, 1:2] - mean * mean + epsilon)
        t_mean = stats[:, 2:3]
        tn_mean = inverse * (stats[:, 3:4] - mean * t_mean)
        normed = (att_ref[where, :] - mean) * inverse
        gating = act_ref[where, 0:width].astype(F32)
        gated = (normed * gating).astype(BF16)
        mixed_ref[rows_at(out_at * ROWS, ROWS), :] = mm(gated, wout_ref[...]).astype(
            mixed_ref.dtype
        )
        gated_grad = mm_rt(g_ref[where, :], wout_ref[...])
        t_rows = gated_grad * gating
        below = at * ROWS + lax.broadcasted_iota(jnp.int32, (ROWS, width), 0) < length
        datt = jnp.where(below, (t_rows - t_mean - normed * tn_mean) * inverse, 0.0)
        datt_ref[where, :] = datt.astype(BF16)
        pre = mm(x_ref[where, :], w_ref[:, 0:width])
        dgate = jnp.where(below, gated_grad * normed * slope_of(pre), 0.0)
        dgate_ref[where, :] = dgate.astype(BF16)

    def middles(at, carry):
        middle((1 - mine) * (count // ROWS) + at, at, mixed_o_ref)
        middle(mine * (count // ROWS) + at, at, mixed_m_ref)
        return carry

    lax.fori_loop(0, count // ROWS, middles, 0)
    scale = HEAD ** (-0.5)
    dq_ref[...] = jnp.zeros_like(dq_ref)

    def head_cols(kind, head):
        return pl.ds(kind * width + head * HEAD, HEAD)

    def pair(query, grad, keys, values, ok):
        scaled = mm_rt(keys, query) * scale
        value, above = silu_parts(scaled)
        weights_grad = mm_rt(values, grad)
        score_grad = weights_grad * above * (1.0 + scaled - value)
        if ok is not None:
            value = jnp.where(ok, value, 0.0)
            score_grad = jnp.where(ok, score_grad, 0.0)
        score_grad = score_grad.astype(BF16)
        return (
            mm(value.astype(BF16), grad),
            mm(score_grad, query),
            mm_lt(score_grad, keys),
        )

    def back(key_at, carry):
        heads = range(width // HEAD)
        keys_here = rows_at(key_at * BLOCK, BLOCK)
        keys = [act_ref[keys_here, head_cols(3, head)] for head in heads]
        values = [act_ref[keys_here, head_cols(1, head)] for head in heads]
        ok = lax.broadcasted_iota(jnp.int32, (BLOCK, BLOCK), 0) <= (
            lax.broadcasted_iota(jnp.int32, (BLOCK, BLOCK), 1)
        )

        def visit(at, sums, ok=None):
            where = rows_at(at * BLOCK, BLOCK)
            new = []
            for head in heads:
                more_v, more_k, more_q = pair(
                    act_ref[where, head_cols(2, head)],
                    datt_ref[where, head_cols(0, head)],
                    keys[head],
                    values[head],
                    ok,
                )
                dq_ref[where, head_cols(0, head)] += more_q
                new += [sums[2 * head] + more_v, sums[2 * head + 1] + more_k]
            return tuple(new)

        zero = tuple(jnp.zeros((BLOCK, HEAD), F32) for _ in range(2 * len(heads)))
        sums = visit(key_at, zero, ok)
        sums = lax.fori_loop(key_at + 1, total // BLOCK, visit, sums)
        for head in heads:
            dv_ref[keys_here, head_cols(0, head)] = sums[2 * head]
            dk_ref[keys_here, head_cols(0, head)] = sums[2 * head + 1]
        return carry

    lax.fori_loop(0, total // BLOCK, back, 0)

    def finish(at, out_at, gx_ref):
        where = rows_at(at * ROWS, ROWS)
        slope = slope_of(mm(x_ref[where, :], w_ref[:, width:]))
        factor = 0.5 * scale
        grads = jnp.concatenate(
            [
                dgate_ref[where, :],
                (dv_ref[where, :] * slope[:, 0:width]).astype(BF16),
                (dq_ref[where, :] * factor * slope[:, width : 2 * width]).astype(BF16),
                (dk_ref[where, :] * factor * slope[:, 2 * width :]).astype(BF16),
            ],
            axis=1,
        )
        gx_ref[rows_at(out_at * ROWS, ROWS), :] = mm_rt(grads, w_ref[...]).astype(gx_ref.dtype)

    def finishes(at, carry):
        finish((1 - mine) * (count // ROWS) + at, at, gx_o_ref)
        finish(mine * (count // ROWS) + at, at, gx_m_ref)
        return carry

    lax.fori_loop(0, count // ROWS, finishes, 0)


def scatter_body(place_ref, slots_ref, embedded_ref, g_ref, gx_m_ref, gx_o_ref, out_ref, grads, hot):
    count = embedded_ref.shape[0]
    first = place_ref[0] * count

    def embed_back(at, carry):
        where = rows_at(at * ROWS, ROWS)
        normed, inverse = normalize(embedded_ref[where, :])
        grad_x = gx_m_ref[where, :].astype(F32) + gx_o_ref[where, :].astype(F32)
        back = (
            grad_x
            - jnp.mean(grad_x, axis=-1, keepdims=True)
            - normed * jnp.mean(grad_x * normed, axis=-1, keepdims=True)
        ) * inverse
        below = (
            first + at * ROWS + lax.broadcasted_iota(jnp.int32, back.shape, 0) < place_ref[1]
        )
        grads[where, :] = jnp.where(below, g_ref[where, :].astype(F32) + back, 0.0).astype(BF16)
        return carry

    lax.fori_loop(0, count // ROWS, embed_back, 0)
    places = lax.broadcasted_iota(jnp.int32, (ROWS, HEAD), 0)

    def step(at, carry):
        here = places + at * ROWS
        for part in range(count // HEAD):
            cols = slice(part * HEAD, (part + 1) * HEAD)
            total = jnp.zeros((ROWS, HEAD), F32)
            for feature in range(slots_ref.shape[0]):
                total = total + jnp.where(slots_ref[feature : feature + 1, cols] == here, 1.0, 0.0)
            hot[:, cols] = total.astype(BF16)
        out_ref[rows_at(at * ROWS, ROWS), :] = mm(hot[...], grads[...]).astype(BF16)
        return carry

    lax.fori_loop(0, out_ref.shape[0] // ROWS, step, 0)


def owner_body(place_ref, ids_ref, returned_ref, mine_ref, other_ref, hot):
    count = mine_ref.shape[0]
    places = lax.broadcasted_iota(jnp.int32, (ROWS, HEAD), 0)

    def rows_of(at, out_at, out_ref):
        here = places + at * ROWS
        for part in range(ids_ref.shape[0] * ids_ref.shape[1] // HEAD):
            row, col = divmod(part * HEAD, ids_ref.shape[1])
            hit = ids_ref[row : row + 1, col : col + HEAD] == here
            hot[:, part * HEAD : (part + 1) * HEAD] = jnp.where(hit, 1.0, 0.0).astype(BF16)
        out_ref[rows_at(out_at * ROWS, ROWS), :] = mm(hot[...], returned_ref[...]).astype(
            out_ref.dtype
        )

    def step(at, carry):
        rows_of((1 - place_ref[0]) * (count // ROWS) + at, at, other_ref)
        rows_of(place_ref[0] * (count // ROWS) + at, at, mine_ref)
        return carry

    lax.fori_loop(0, count // ROWS, step, 0)


def swap(array):
    return lax.ppermute(array, "ctx", [(0, 1), (1, 0)])


def on_device(item_table, serve_rows, token_slots, lengths, w_proj, w_out, grad_out):
    table_rows, row_width = item_table.shape
    requesters, asked = serve_rows.shape
    slot_total = requesters * asked
    row_count, features = token_slots.shape[1:]
    hidden_full = w_out.shape[0]
    shards = lax.axis_size("ctx")
    assert shards == 2
    total = row_count * shards
    mine = lax.axis_index("ctx")
    place = jnp.stack([mine, lengths[0]])
    shape = jax.ShapeDtypeStruct

    cotangent = grad_out[0]
    cotangent_o = swap(cotangent)
    ids = serve_rows.reshape(-1, BLOCK)
    served = call(
        serve_body,
        shape((slot_total, row_width), BF16),
        [vmem(), vmem()],
        [pltpu.VMEM((table_rows, row_width), BF16), pltpu.VMEM((BLOCK, table_rows), BF16)],
        flops=2 * slot_total * table_rows * row_width,
        moved=4 * table_rows * row_width,
    )(ids, item_table)
    fetched = lax.all_to_all(
        served.reshape(requesters, asked, row_width),
        "table",
        split_axis=0,
        concat_axis=0,
        tiled=True,
    ).reshape(slot_total, row_width)
    slots = token_slots[0].T
    embedded, normed = call(
        embed_body,
        (shape((row_count, row_width), F32), shape((row_count, row_width), BF16)),
        [vmem(), vmem()],
        [pltpu.VMEM((ROWS, slot_total), BF16)],
        flops=2 * slot_total * row_count * row_width,
        moved=2 * slot_total * row_width,
    )(slots, fetched)

    head_total = hidden_full // HEAD
    share = head_total // shards
    width = share * HEAD
    proj_cols = lax.dynamic_slice_in_dim(
        w_proj.reshape(row_width, 4, head_total, HEAD), mine * share, share, 2
    ).reshape(row_width, 4 * width)
    out_rows = lax.dynamic_slice_in_dim(
        w_out.reshape(head_total, HEAD, row_width), mine * share, share, 0
    ).reshape(width, row_width)

    normed_o = swap(normed)
    x_all, g_all, act, attended, stats = call(
        forward_body,
        (
            shape((total, row_width), BF16),
            shape((total, row_width), BF16),
            shape((total, 4 * width), BF16),
            shape((total, width), F32),
            shape((8, total), F32),
        ),
        [smem()] + [vmem()] * 6,
        flops=2 * total * total * width + 8 * total * row_width * width,
        moved=12 * total * width,
    )(place, normed, normed_o, cotangent, cotangent_o, proj_cols, out_rows)
    stats_o = swap(stats)
    part = shape((row_count, row_width), BF16)
    mixed_m, mixed_o, gx_m, gx_o = call(
        backward_body,
        (shape((row_count, row_width), F32), part, shape((row_count, row_width), F32), part),
        [smem()] + [vmem()] * 8,
        [
            pltpu.VMEM((total, width), BF16),
            pltpu.VMEM((total, width), BF16),
            pltpu.VMEM((total, width), F32),
            pltpu.VMEM((total, width), F32),
            pltpu.VMEM((total, width), F32),
        ],
        flops=5 * total * total * width + 16 * total * row_width * width,
        moved=12 * total * width,
    )(place, x_all, g_all, act, attended, stats, stats_o, proj_cols, out_rows)
    gx_in = swap(gx_o)
    mixed_in = swap(mixed_o)
    slot_grads = call(
        scatter_body,
        shape((slot_total, row_width), BF16),
        [smem()] + [vmem()] * 5,
        [pltpu.VMEM((row_count, row_width), BF16), pltpu.VMEM((ROWS, row_count), BF16)],
        flops=2 * slot_total * row_count * row_width,
        moved=2 * slot_total * row_width,
    )(place, slots, embedded, cotangent, gx_m, gx_in)
    returned = lax.all_to_all(
        slot_grads.reshape(requesters, asked, row_width),
        "table",
        split_axis=0,
        concat_axis=0,
        tiled=True,
    ).reshape(slot_total, row_width)
    half_rows = table_rows // shards
    owner_m, owner_o = call(
        owner_body,
        (shape((half_rows, row_width), F32), shape((half_rows, row_width), BF16)),
        [smem()] + [vmem()] * 2,
        [pltpu.VMEM((ROWS, slot_total), BF16)],
        flops=2 * slot_total * table_rows * row_width,
        moved=2 * slot_total * row_width,
    )(place, ids, returned)
    grad_table = owner_m + swap(owner_o).astype(F32)
    positions = mine * row_count + jnp.arange(row_count, dtype=jnp.int32)
    layer_out = jnp.where(
        (positions < lengths[0])[:, None], embedded + (mixed_m + mixed_in.astype(F32)), 0.0
    ).astype(BF16)
    return (layer_out[None], grad_table)


def solution(mesh):
    placed = (
        P("table", None),
        P("table", "ctx"),
        P("table", "ctx", None),
        P("table"),
        P(),
        P(),
        P("table", "ctx", None),
    )
    return jax.shard_map(
        on_device,
        mesh=mesh,
        in_specs=placed,
        out_specs=(P("table", "ctx", None), P(("table", "ctx"), None)),
        check_vma=False,
    )
```

time: 509 us -> 233 us (0.46)
  other arithmetic: 111 us -> 4.09 us
  Pallas kernels: 0 us -> 105 us
  matrix products: 99.8 us -> 0 us
  local copies, waits for them, and re-layouts: 88.2 us -> 9.39 us
  waiting for transfers between devices: 172 us -> 97.1 us
  between operations: 14.8 us -> 1.35 us
  blocking collectives: 6.74 us -> 0 us
    pallas_call x0 -> x6, Pallas kernels: none -> 105 us  [the longest x1 34.9 us: on_device(): call(backward_body, (shape((row_count, row_width), F32), part, shape((row...]
    dot_general x28 -> x0, matrix products: 99.8 us -> none  [the longest x4 30.4 us: attend_all(): jnp.einsum('hij,jhd->ihd', weights, split_heads(value_block), preferred_e...]
    all_to_all x2, waiting for transfers between devices: 142 us -> 93.7 us  [the longest x1 47.3 us: on_device(): lax.all_to_all(slot_grads.reshape(requesters, asked, row_width), 'table',...]
    scatter-add x2 -> x0, other arithmetic: 47.5 us -> none  [the longest x1 25 us: on_device(): jax.ops.segment_sum(spread, slot_ids.reshape(-1), num_segments=fetched_ro...]
    gather x5 -> x0, local copies, waits for them, and re-layouts: 40 us -> none  [the longest x3 16.9 us: on_device(): embedded = embedded + fetched_rows[slot_ids[:, feature]]]
    convert_element_type x12 -> x0, other arithmetic: 31.2 us -> none  [the longest x8 21.5 us: allowed(): ((key_pos[None, :] <= query_pos[:, None]) & (key_pos[None, :] < length))....]
    reduce_scatter x3 -> x0, waiting for transfers between devices: 25 us -> none  [the longest x1 9.92 us: on_device(): lax.psum_scatter(jnp.dot(gated_m, out_rows, preferred_element_type=jnp.fl...]
    dynamic_slice x13 -> x1, local copies, waits for them, and re-layouts: 14.9 us -> 0.66 us  [on_device(): lax.dynamic_slice_in_dim(w_out.reshape(head_total, HEAD, row_width), mine...]
  transfers between devices with their start and end apart: 7 -> 8, of which waited for: 6 -> 4; matrix products, arithmetic and copies ran while one was open for 16% -> 3% of each run, Pallas kernels for 0% -> 10%
where the time goes in v1:
time: 233 us
  Pallas kernels  105 us (45%)
  waiting for transfers between devices  97.1 us (42%)
  starting transfers between devices  16 us (7%)
  local copies, waits for them, and re-layouts  9.39 us (4%)
  other arithmetic  4.09 us (2%)
    all_to_all x1, waiting for transfers between devices, on_device(): lax.all_to_all(slot_grads.reshape(requesters, asked, row_width), 'table',...  47.3 us
    all_to_all x1, waiting for transfers between devices, on_device(): lax.all_to_all(served.reshape(requesters, asked, row_width), 'table', spl...  46.5 us
    pallas_call x1, Pallas kernels, on_device(): call(backward_body, (shape((row_count, row_width), F32), part, shape((row...  34.9 us
    pallas_call x1, Pallas kernels, on_device(): call(forward_body, (shape((total, row_width), BF16), shape((total, row_wi...  20.1 us
    pallas_call x1, Pallas kernels, on_device(): call(scatter_body, shape((slot_total, row_width), BF16), [smem()] + [vmem...  15.2 us
    pallas_call x1, Pallas kernels, on_device(): call(embed_body, (shape((row_count, row_width), F32), shape((row_count, r...  14.6 us
    pallas_call x1, Pallas kernels, on_device(): call(serve_body, shape((slot_total, row_width), BF16), [vmem(), vmem()],...  10 us
    pallas_call x1, Pallas kernels, on_device(): call(owner_body, (shape((half_rows, row_width), F32), shape((half_rows, r...  9.75 us
  transfers between devices with their start and end apart: 8, of which 4 were waited for; matrix products, arithmetic and copies ran while one was open for 3% of the time, Pallas kernels for 10%

profile of v1, /device:TPU:15, one launch (start us, length us, event | category | flops | bytes accessed | tf_op | source)
XLA Modules:
  0.0 232.6 jit_solution(17862541407043951692)
XLA Ops:
  0.6 0.0 copy-start
  0.6 1.4 reshape.36.ids_ref
  2.0 10.0 %shard_map.86 = bf16[4096,256]{1,0:T(8,128)(2,1)} custom-call(s32[8,512]{1,0:T(8,128)} %reshape.36.ids_ref, f32[2048,256]{1,0:T(8,128)} %table_ref.1), custom_call_target="tpu_custom_call" | custom-call | flops 4294967296 | bytes 2097152 | tf_op jit(solution)/shard_map/pallas_call | solution.py:394
  12.0 6.6 %all-to-all-start = ((bf16[16,256,256]{2,1,0:T(8,128)(2,1)}), bf16[16,256,256]{2,1,0:T(8,128)(2,1)S(1)}, u32[]{:S(2)}, u32[]{:S(2)}) async-start(bf16[16,256,256]{2,1,0:T(8,128)(2,1)} %bitcast.19), calls=%async_computation | async-start | bytes 4194304 | tf_op jit(solution)/shard_map/all_to_all | solution.py:402
  18.6 1.2 collective-permute-start.1
  19.8 46.5 %all-to-all-done = bf16[16,256,256]{2,1,0:T(8,128)(2,1)S(1)} async-done(((bf16[16,256,256]{2,1,0:T(8,128)(2,1)}), bf16[16,256,256]{2,1,0:T(8,128)(2,1)S(1)}, u32[]{:S(2)}, u32[]{:S(2)}) %all-to-all-start) | async-done | bytes 2097184 | tf_op jit(solution)/shard_map/all_to_all | solution.py:402
  66.3 1.3 copy-done.2
  67.6 14.6 %shard_map.87 = (f32[1024,256]{1,0:T(8,128)}, bf16[1024,256]{1,0:T(8,128)(2,1)}) custom-call(s32[4,1024]{1,0:T(4,128)} %bitcast.22, bf16[4096,256]{1,0:T(8,128)(2,1)} %bitcast.17), custom_call_target="tpu_custom_call" | custom-call | flops 2147483648 | bytes 2097152 | tf_op jit(solution)/shard_map/pallas_call | solution.py:410
  82.3 1.4 collective-permute-start
  84.3 0.8 reshape.39
  85.1 0.5 constant_dynamic-slice_fusion.1
  85.7 1.2 reshape.40.w_ref
  86.8 0.6 pad_add_fusion.place_ref
  87.5 0.7 constant_dynamic-slice_fusion
  88.2 0.8 copy-done.6
  89.0 20.1 %shard_map.88 = (bf16[2048,256]{1,0:T(8,128)(2,1)}, bf16[2048,256]{1,0:T(8,128)(2,1)}, bf16[2048,1024]{1,0:T(8,128)(2,1)}, f32[2048,256]{1,0:T(8,128)}, f32[8,2048]{1,0:T(8,128)}) custom-call(s32[2]{0:T(128)} %pad_add_fusion.place_ref, bf16[1024,256]{1,0:T(8,128)(2,1)} %get-tuple-element.16.xm_ref, bf16[1024,256]{1,0:T(8,128)(2,1)} %copy-done.6, ...), custom_call_target="tpu_custom_call" | custom-call | flops 3221225472 | bytes 6291456 | tf_op jit(solution)/shard_map/pallas_call | solution.py:430
  109.1 0.0 collective-permute-start.2
  109.1 1.5 collective-permute-done.2.stats_o_ref
  110.5 0.6 copy-done.8
  111.2 34.9 %shard_map.89 = (f32[1024,256]{1,0:T(8,128)}, bf16[1024,256]{1,0:T(8,128)(2,1)}, f32[1024,256]{1,0:T(8,128)}, bf16[1024,256]{1,0:T(8,128)(2,1)}) custom-call(s32[2]{0:T(128)} %pad_add_fusion.place_ref, bf16[2048,256]{1,0:T(8,128)(2,1)} %get-tuple-element.17.x_ref, bf16[2048,256]{1,0:T(8,128)(2,1)} %get-tuple-element.18.g_ref, ...), custom_call_target="tpu_custom_call" | custom-call | flops 7516192768 | bytes 6291456 | tf_op jit(solution)/shard_map/pallas_call | solution.py:445
  146.0 0.2 collective-permute-start.4
  146.2 2.0 collective-permute-done.4.gx_o_ref
  148.2 0.8 copy-done.7
  148.9 15.2 %shard_map.90 = bf16[4096,256]{1,0:T(8,128)(2,1)} custom-call(s32[2]{0:T(128)} %pad_add_fusion.place_ref, s32[4,1024]{1,0:T(4,128)} %bitcast.23, f32[1024,256]{1,0:T(8,128)} %get-tuple-element.15.embedded_ref, bf16[1024,256]{1,0:T(8,128)(2,1)} %bitcast.6.gm_ref.g_ref, f32[1024,256]{1,0:T(8,128)} %get-tuple-element.24.gx_m_ref, bf16[1024,256]{1,0:T(8,128)(2,1)} %copy-done.7), custom_call_target="tpu_custom_call" | custom-call | flops 2147483648 | bytes 2097152 | tf_op jit(solution)/shard_map/pallas_call | solution.py:461
  164.2 4.6 %all-to-all-start.1 = ((bf16[16,256,256]{2,1,0:T(8,128)(2,1)}), bf16[16,256,256]{2,1,0:T(8,128)(2,1)S(1)}, u32[]{:S(2)}, u32[]{:S(2)}) async-start(bf16[16,256,256]{2,1,0:T(8,128)(2,1)} %bitcast.18), calls=%async_computation.1 | async-start | bytes 4194304 | tf_op jit(solution)/shard_map/all_to_all | solution.py:469
  168.8 0.7 collective-permute-start.3
  169.5 47.3 %all-to-all-done.1 = bf16[16,256,256]{2,1,0:T(8,128)(2,1)S(1)} async-done(((bf16[16,256,256]{2,1,0:T(8,128)(2,1)}), bf16[16,256,256]{2,1,0:T(8,128)(2,1)S(1)}, u32[]{:S(2)}, u32[]{:S(2)}) %all-to-all-start.1) | async-done | bytes 2097184 | tf_op jit(solution)/shard_map/all_to_all | solution.py:469
  216.8 1.3 copy-done.1
  218.1 9.8 %shard_map.91 = (f32[1024,256]{1,0:T(8,128)}, bf16[1024,256]{1,0:T(8,128)(2,1)}) custom-call(s32[2]{0:T(128)} %pad_add_fusion.place_ref, s32[8,512]{1,0:T(8,128)} %reshape.36.ids_ref, bf16[4096,256]{1,0:T(8,128)(2,1)} %bitcast.16), custom_call_target="tpu_custom_call" | custom-call | flops 4294967296 | bytes 2097152 | tf_op jit(solution)/shard_map/pallas_call | solution.py:477
  227.8 1.3 collective-permute-start.5
  229.2 2.4 %fusion = bf16[1,1024,256]{2,1,0:T(8,128)(2,1)} fusion(f32[1024,256]{1,0:T(8,128)S(1)} %copy-done.4, f32[1024,256]{1,0:T(8,128)} %get-tuple-element.22, bf16[1024,256]{1,0:T(8,128)(2,1)} %collective-permute-done.3, pred[1024]{0:T(1024)(128)(4,1)S(1)} %add_compare_fusion), kind=kLoop, calls=%fused_computation.2 | loop fusion | flops 1310720 | bytes 3146752 | tf_op jit(solution)/shard_map/broadcast_in_dim | solution.py:490
  231.5 1.1 convert_add_fusion
  (17 shorter events, 0.0 us)
Async XLA Ops:
  0.6 86.9 %copy-start = (bf16[512,256]{1,0:T(8,128)(2,1)S(1)}, bf16[512,256]{1,0:T(8,128)(2,1)}, u32[]{:S(2)}) copy-start(bf16[512,256]{1,0:T(8,128)(2,1)} %param.12) | copy-start | bytes 786436
  12.0 54.3 %all-to-all-start = ((bf16[16,256,256]{2,1,0:T(8,128)(2,1)}), bf16[16,256,256]{2,1,0:T(8,128)(2,1)S(1)}, u32[]{:S(2)}, u32[]{:S(2)}) async-start(bf16[16,256,256]{2,1,0:T(8,128)(2,1)} %bitcast.19), calls=%async_computation | async-start | bytes 4194304 | tf_op jit(solution)/shard_map/all_to_all | solution.py:402
  18.6 69.6 %collective-permute-start.1 = (bf16[1024,256]{1,0:T(8,128)(2,1)}, bf16[1024,256]{1,0:T(8,128)(2,1)}, u32[]{:S(2)}, u32[]{:S(2)}) collective-permute-start(bf16[1024,256]{1,0:T(8,128)(2,1)} %bitcast.6.gm_ref.g_ref), channel_id=1, source_target_pairs={{0,1},{1,0},{2,3},{3,2},{4,5},{5,4},{6,7},{7,6},{8,9},{9,8},{10,11... | collective-permute-start | bytes 1572872 | tf_op jit(solution)/shard_map/ppermute | solution.py:375
  66.3 1.3 copy-start.2
  67.6 16.7 %copy-start.3 = (bf16[256,2048]{1,0:T(8,128)(2,1)S(1)}, bf16[256,2048]{1,0:T(8,128)(2,1)}, u32[]{:S(2)}) copy-start(bf16[256,2048]{1,0:T(8,128)(2,1)} %param.11) | copy-start | bytes 3145732
  82.3 5.9 %collective-permute-start = (bf16[1024,256]{1,0:T(8,128)(2,1)}, bf16[1024,256]{1,0:T(8,128)(2,1)S(1)}, u32[]{:S(2)}, u32[]{:S(2)}) collective-permute-start(bf16[1024,256]{1,0:T(8,128)(2,1)} %get-tuple-element.16.xm_ref), channel_id=1, source_target_pairs={{0,1},{1,0},{2,3},{3,2},{4,5},{5,4},{6,7},{7,6},{8,9},{9,8},{10,11... | collective-permute-start | bytes 1572872 | tf_op jit(solution)/shard_map/ppermute | solution.py:375
  88.2 0.8 copy-start.6
  109.1 1.5 collective-permute-start.2
  110.5 0.6 copy-start.8
  146.0 2.1 collective-permute-start.4
  148.1 0.8 copy-start.7
  164.2 52.6 %all-to-all-start.1 = ((bf16[16,256,256]{2,1,0:T(8,128)(2,1)}), bf16[16,256,256]{2,1,0:T(8,128)(2,1)S(1)}, u32[]{:S(2)}, u32[]{:S(2)}) async-start(bf16[16,256,256]{2,1,0:T(8,128)(2,1)} %bitcast.18), calls=%async_computation.1 | async-start | bytes 4194304 | tf_op jit(solution)/shard_map/all_to_all | solution.py:469
  168.8 60.4 %collective-permute-start.3 = (bf16[1024,256]{1,0:T(8,128)(2,1)}, bf16[1024,256]{1,0:T(8,128)(2,1)}, u32[]{:S(2)}, u32[]{:S(2)}) collective-permute-start(bf16[1024,256]{1,0:T(8,128)(2,1)} %get-tuple-element.23), channel_id=1, source_target_pairs={{0,1},{1,0},{2,3},{3,2},{4,5},{5,4},{6,7},{7,6},{8,9},{9,8},{10,11... | collective-permute-start | bytes 1572872 | tf_op jit(solution)/shard_map/ppermute | solution.py:375
  216.8 1.3 copy-start.1
  218.1 11.1 %copy-start.4 = (f32[1024,256]{1,0:T(8,128)S(1)}, f32[1024,256]{1,0:T(8,128)}, u32[]{:S(2)}) copy-start(f32[1024,256]{1,0:T(8,128)} %get-tuple-element.15.embedded_ref) | copy-start | bytes 3145732
  227.8 3.7 %copy-start.5 = (f32[1024,256]{1,0:T(8,128)S(1)}, f32[1024,256]{1,0:T(8,128)}, u32[]{:S(2)}) copy-start(f32[1024,256]{1,0:T(8,128)} %get-tuple-element.26) | copy-start | bytes 3145732
  227.8 3.7 %collective-permute-start.5 = (bf16[1024,256]{1,0:T(8,128)(2,1)}, bf16[1024,256]{1,0:T(8,128)(2,1)S(1)}, u32[]{:S(2)}, u32[]{:S(2)}) collective-permute-start(bf16[1024,256]{1,0:T(8,128)(2,1)} %get-tuple-element.27), channel_id=1, source_target_pairs={{0,1},{1,0},{2,3},{3,2},{4,5},{5,4},{6,7},{7,6},{8,9},{9,8},{10,11... | collective-permute-start | bytes 1572872 | tf_op jit(solution)/shard_map/ppermute | solution.py:375
